TPU v7x, 512 devices: a whole 4x8x8 slice. The times are simulated.
512 devices in a mesh: pages: 64 (over y, z_lo, core), heads: 8 (over x, z_hi).
Axes of the slice: x: 4, y: 8, z: 8 (z_hi: 2, z_lo: 4; z = z_hi * 4 + z_lo), core: 2. Of those that a mesh axis runs over, the one named last changes fastest.
Arguments:
- candidates: bfloat16 [49152, 1024], P(('pages', 'heads')), may hold values from -6 to 6
- in_weight: bfloat16 [2, 1024, 8, 512], P(None, None, 'heads'), may hold values from -0.1875 to 0.1875
- out_weight: bfloat16 [2, 8, 128, 1024], P(None, 'heads'), may hold values from -0.1875 to 0.1875
- page_cache: bfloat16 [2, 4096, 8, 2, 32, 128], P(None, 'pages', 'heads'), may hold values from -6 to 6
- page_lists: int32 [1024, 4], P('pages'), may hold values from 0 to 4095, as said below
- hist_len: int32 [1024], P('pages'), may hold values from 1 to 128
Outputs:
- hidden_out: bfloat16 [49152, 1024], P(('pages', 'heads'))
Inputs may be any that keep to these rules, and one draw needn't show every extreme that they name: `page_lists`: every page id appears in exactly one list. Page p lies on index p // 64 of pages; the requests of one index of pages list either none or exactly 2 pages that lie on any one index.
All inputs are finite; a program needn't handle non-finite values.
Results may differ from a plain program's by a relative error of at most 0.018.
Values may be sent and summed in bfloat16 or wider, within the bound.
A program may use at most 64 MiB of HBM per device.

v0:
```python
import math
import jax
import jax.numpy as jnp
from jax import lax
from jax.sharding import PartitionSpec as P

eps = 1e-05


def layer_norm(values):
    row_mean = jnp.mean(values, -1, keepdims=True)
    centred = values - row_mean
    spread = jnp.mean(centred * centred, -1, keepdims=True)
    return centred * lax.rsqrt(spread + eps)


def gather_rows(rows):
    return lax.all_gather(rows, "heads", axis=0, tiled=True)


def scatter_sum(terms):
    return lax.psum_scatter(terms, "heads", scatter_dimension=0, tiled=True).astype(jnp.float32)


def on_device(candidates, in_weight, out_weight, page_cache, page_lists, hist_len):
    readers = lax.axis_size("pages")
    head_group = lax.axis_size("heads")
    layers = in_weight.shape[0]
    model_width = in_weight.shape[1]
    head_dim = out_weight.shape[2]
    pages_here = page_cache.shape[1]
    page_len = page_cache.shape[4]
    requests, max_pages = page_lists.shape
    slot_count = requests * max_pages
    capacity = 2 * slot_count // readers
    cand_rows = candidates.shape[0] * head_group
    per_request = cand_rows // requests
    history = max_pages * page_len
    score_scale = 1.0 / math.sqrt(head_dim)
    flat_ids = page_lists.reshape(slot_count)
    slot_owner = flat_ids // pages_here
    local_ids = flat_ids % pages_here
    slot_order = jnp.arange(slot_count)
    earlier_same = (slot_owner[None, :] == slot_owner[:, None]) & (
        slot_order[None, :] < slot_order[:, None]
    )
    slot_rank = jnp.sum(earlier_same.astype(jnp.int32), axis=1)
    places = slot_owner * capacity + slot_rank
    matches = places[None, :] == jnp.arange(readers * capacity)[:, None]
    asked = jnp.sum(jnp.where(matches, local_ids[None, :], 0), axis=1)
    wanted = lax.all_to_all(
        asked.reshape(readers, capacity), "pages", split_axis=0, concat_axis=0, tiled=True
    ).reshape(readers * capacity)
    histories = []
    for layer_index in range(layers):
        sent = jnp.take(page_cache[layer_index, :, 0], wanted, axis=0)
        if histories:
            sent, histories[-1] = lax.optimization_barrier((sent, histories[-1]))
        histories.append(
            lax.all_to_all(
                sent.reshape((readers, capacity) + sent.shape[1:]),
                "pages",
                split_axis=0,
                concat_axis=0,
                tiled=True,
            )
        )
    divisors = (hist_len + 1).astype(jnp.float32)
    cand_divisors = jnp.repeat(divisors, per_request)
    live = jnp.arange(history)[None, :] < hist_len[:, None]
    hidden_rows = candidates
    for layer_index in range(layers):
        weights_in = in_weight[layer_index].reshape(model_width, 4 * head_dim)
        ready = layer_norm(gather_rows(hidden_rows).astype(jnp.float32)).astype(jnp.bfloat16)
        projected = jax.nn.silu(jnp.dot(ready, weights_in, preferred_element_type=jnp.float32))
        gate_part = projected[:, :head_dim]
        value_part = projected[:, head_dim : 2 * head_dim].astype(jnp.bfloat16)
        query_part = projected[:, 2 * head_dim : 3 * head_dim].astype(jnp.bfloat16)
        key_part = projected[:, 3 * head_dim :].astype(jnp.bfloat16)
        got, query_part = lax.optimization_barrier((histories[layer_index], query_part))
        got = got.reshape(readers * capacity, 2, page_len, head_dim)
        listed = jnp.take(got, places, axis=0).reshape(requests, max_pages, 2, page_len, head_dim)
        hist_keys = listed[:, :, 0].reshape(requests, history, head_dim)
        hist_values = listed[:, :, 1].reshape(requests, history, head_dim)
        queries = query_part.reshape(requests, per_request, head_dim)
        scores = (
            jnp.einsum("rqd,rtd->rqt", queries, hist_keys, preferred_element_type=jnp.float32)
            * score_scale
        )
        weights = (
            jnp.where(live[:, None, :], jax.nn.silu(scores), 0.0) / divisors[:, None, None]
        ).astype(jnp.bfloat16)
        attended = jnp.einsum(
            "rqt,rtd->rqd", weights, hist_values, preferred_element_type=jnp.float32
        ).reshape(cand_rows, head_dim)
        self_score = (
            jnp.sum(query_part.astype(jnp.float32) * key_part.astype(jnp.float32), -1) * score_scale
        )
        self_weight = (jax.nn.silu(self_score) / cand_divisors).astype(jnp.bfloat16)
        attended = attended + self_weight.astype(jnp.float32)[:, None] * value_part.astype(
            jnp.float32
        )
        gated_rows = (layer_norm(attended) * gate_part).astype(jnp.bfloat16)
        weights_out = out_weight[layer_index].reshape(head_dim, model_width)
        terms = jnp.dot(gated_rows, weights_out, preferred_element_type=jnp.float32)
        summed = scatter_sum(terms.astype(jnp.bfloat16))
        hidden_rows = (hidden_rows.astype(jnp.float32) + summed).astype(jnp.bfloat16)
    return hidden_rows


def solution(mesh):
    in_specs = (
        P(("pages", "heads"), None),
        P(None, None, "heads", None),
        P(None, "heads", None, None),
        P(None, "pages", "heads", None, None, None),
        P("pages", None),
        P("pages"),
    )
    out_specs = P(("pages", "heads"), None)
    return jax.shard_map(
        on_device, mesh=mesh, in_specs=in_specs, out_specs=out_specs, check_vma=False
    )
```

profile of v0, /device:TPU:8, one launch (start us, length us, event | category | flops | bytes accessed | tf_op | source)
XLA Modules:
  0.0 485.0 jit_solution(15698231655504196997)
XLA Ops:
  6.5 0.8 copy.31
  7.7 0.8 all_to_all.12
  8.5 13.5 %all-to-all-start = ((s32[64,1,2]{2,1,0:T(1,128)}), s32[64,1,2]{2,1,0:T(1,128)S(1)}, u32[]{:S(2)}, u32[]{:S(2)}) async-start(s32[64,1,2]{2,1,0:T(1,128)} %bitcast), calls=%async_computation | async-start | bytes 65536 | tf_op jit(solution)/shard_map/all_to_all | solution.py:51
  22.0 2.0 slice_bitcast_fusion
  24.0 6.8 %all-to-all-done = s32[64,1,2]{2,1,0:T(1,128)S(1)} async-done(((s32[64,1,2]{2,1,0:T(1,128)}), s32[64,1,2]{2,1,0:T(1,128)S(1)}, u32[]{:S(2)}, u32[]{:S(2)}) %all-to-all-start) | async-done | bytes 544 | tf_op jit(solution)/shard_map/all_to_all | solution.py:51
  32.2 2.2 gather_fusion
  34.4 2.1 gather_fusion.1
  36.5 4.0 broadcast_select_fusion
  40.5 5.8 %all-to-all-start.1 = ((bf16[64,2,2,32,128]{4,3,2,1,0:T(8,128)(2,1)}), bf16[64,2,2,32,128]{4,3,2,1,0:T(8,128)(2,1)S(1)}, u32[]{:S(2)}, u32[]{:S(2)}) async-start(bf16[64,2,2,32,128]{4,3,2,1,0:T(8,128)(2,1)} %bitcast.3), calls=%async_computation.1 | async-start | bytes 4194304 | tf_op jit(solution)/shard_map/all_to_all | solution.py:60
  47.3 104.0 %all-gather.3.cloned.1.call-done = bf16[768,1024]{1,0:T(8,128)(2,1)} async-done(((bf16[96,1024]{1,0:T(8,128)(2,1)}), bf16[768,1024]{1,0:T(8,128)(2,1)}) %all-gather.3.cloned.1.call-update) | async-done | bytes 1572880 | tf_op jit(solution)/shard_map/all_gather | solution.py:18
  151.3 1.8 convert_reduce_fusion.1
  153.8 3.9 fusion.65
  158.5 0.7 gather_fusion.2
  160.9 2.8 convolution_convert_fusion.1
  163.7 8.5 %all-to-all-start.2 = ((bf16[64,2,2,32,128]{4,3,2,1,0:T(8,128)(2,1)}), bf16[64,2,2,32,128]{4,3,2,1,0:T(8,128)(2,1)S(1)}, u32[]{:S(2)}, u32[]{:S(2)}) async-start(bf16[64,2,2,32,128]{4,3,2,1,0:T(8,128)(2,1)} %bitcast.12), calls=%async_computation.3 | async-start | bytes 4194304 | tf_op jit(solution)/shard_map/all_to_all | solution.py:60
  172.2 124.9 %reduce-scatter.3.cloned.1.call-done = bf16[96,1024]{1,0:T(8,128)(2,1)} async-done(((bf16[768,1024]{1,0:T(8,128)(2,1)}), bf16[96,1024]{1,0:T(8,128)(2,1)}) %reduce-scatter.3.cloned.1.call-update) | async-done | bytes 196624 | tf_op jit(solution)/shard_map/reduce_scatter | solution.py:22
  297.1 1.7 add_convert_fusion.1
  299.0 71.7 %all-gather.5.cloned.1.call-done = bf16[768,1024]{1,0:T(8,128)(2,1)} async-done(((bf16[96,1024]{1,0:T(8,128)(2,1)}), bf16[768,1024]{1,0:T(8,128)(2,1)}) %all-gather.5.cloned.1.call-update) | async-done | bytes 1572880 | tf_op jit(solution)/shard_map/all_gather | solution.py:18
  370.7 1.8 convert_reduce_fusion
  373.2 3.9 fusion.66
  377.9 0.7 gather_fusion.3
  380.3 2.8 convolution_convert_fusion
  383.1 93.7 %reduce-scatter.5.cloned.1.call-done = bf16[96,1024]{1,0:T(8,128)(2,1)} async-done(((bf16[768,1024]{1,0:T(8,128)(2,1)}), bf16[96,1024]{1,0:T(8,128)(2,1)}) %reduce-scatter.5.cloned.1.call-update) | async-done | bytes 196624 | tf_op jit(solution)/shard_map/reduce_scatter | solution.py:22
  476.8 1.7 add_convert_fusion
  (81 shorter events, 9.2 us)
Async XLA Ops:
  8.5 22.3 %all-to-all-start = ((s32[64,1,2]{2,1,0:T(1,128)}), s32[64,1,2]{2,1,0:T(1,128)S(1)}, u32[]{:S(2)}, u32[]{:S(2)}) async-start(s32[64,1,2]{2,1,0:T(1,128)} %bitcast), calls=%async_computation | async-start | bytes 65536 | tf_op jit(solution)/shard_map/all_to_all | solution.py:51
  34.4 2.1 copy-start
  40.5 6.5 %copy-start.11 = (s32[16]{0:T(128)S(1)}, s32[16]{0:T(128)}, u32[]{:S(2)}) copy-start(s32[16]{0:T(128)} %param.15) | copy-start | bytes 196
  40.5 117.2 %all-to-all-start.1 = ((bf16[64,2,2,32,128]{4,3,2,1,0:T(8,128)(2,1)}), bf16[64,2,2,32,128]{4,3,2,1,0:T(8,128)(2,1)S(1)}, u32[]{:S(2)}, u32[]{:S(2)}) async-start(bf16[64,2,2,32,128]{4,3,2,1,0:T(8,128)(2,1)} %bitcast.3), calls=%async_computation.1 | async-start | bytes 4194304 | tf_op jit(solution)/shard_map/all_to_all | solution.py:60
  46.3 105.0 %all-gather.3.cloned.1.call-start = ((), (), s32[]{:S(2)}) async-start(), calls=%async_computation.5 | async-start | bytes 1769472 | tf_op jit(solution)/shard_map/all_gather | solution.py:18
  47.0 250.1 %reduce-scatter.3.cloned.1.call-start = ((), (), s32[]{:S(2)}) async-start(), calls=%async_computation.6 | async-start | bytes 1769472 | tf_op jit(solution)/shard_map/reduce_scatter | solution.py:22
  151.3 1.9 copy-start.1
  157.7 0.9 copy-start.6
  159.6 1.1 copy-start.7
  159.6 1.3 copy-start.9
  163.7 133.4 %copy-start.8 = (bf16[96,1024]{1,0:T(8,128)(2,1)S(1)}, bf16[96,1024]{1,0:T(8,128)(2,1)}, u32[]{:S(2)}) copy-start(bf16[96,1024]{1,0:T(8,128)(2,1)} %param.10) | copy-start | bytes 589828
  163.7 213.3 %all-to-all-start.2 = ((bf16[64,2,2,32,128]{4,3,2,1,0:T(8,128)(2,1)}), bf16[64,2,2,32,128]{4,3,2,1,0:T(8,128)(2,1)S(1)}, u32[]{:S(2)}, u32[]{:S(2)}) async-start(bf16[64,2,2,32,128]{4,3,2,1,0:T(8,128)(2,1)} %bitcast.12), calls=%async_computation.3 | async-start | bytes 4194304 | tf_op jit(solution)/shard_map/all_to_all | solution.py:60
  172.2 198.5 %all-gather.5.cloned.1.call-start = ((), (), s32[]{:S(2)}) async-start(), calls=%async_computation.7 | async-start | bytes 1769472 | tf_op jit(solution)/shard_map/all_gather | solution.py:18
  298.8 178.0 %reduce-scatter.5.cloned.1.call-start = ((), (), s32[]{:S(2)}) async-start(), calls=%async_computation.8 | async-start | bytes 1769472 | tf_op jit(solution)/shard_map/reduce_scatter | solution.py:22
  370.7 1.9 copy-start.2
  377.0 0.9 copy-start.4
  378.9 1.1 copy-start.5
  379.0 1.3 copy-start.10
  380.3 96.5 %copy-start.3 = (bf16[96,1024]{1,0:T(8,128)(2,1)S(1)}, bf16[96,1024]{1,0:T(8,128)(2,1)}, u32[]{:S(2)}) copy-start(bf16[96,1024]{1,0:T(8,128)(2,1)} %add_convert_fusion.1) | copy-start | bytes 589828
Sparse Core Ops, SparseCore 0:
  50.3 101.0 all-gather.2
  163.8 133.2 reduce-scatter.2
  300.3 70.3 all-gather.4
  383.2 93.4 reduce-scatter.4
where the time goes:
time: 486 us; the launch traced here: 485 us
  waiting for transfers between devices  402 us (83%)
  starting transfers between devices  28.1 us (6%)
  matrix products  14.5 us (3%)
  other arithmetic  14 us (3%)
  between operations  13.5 us (3%)
  local copies, waits for them, and re-layouts  13.1 us (3%)
    reduce_scatter x2, waiting for transfers between devices, scatter_sum(): lax.psum_scatter(terms, 'heads', scatter_dimension=0, tiled=True)  219 us
    all_gather x2, waiting for transfers between devices, gather_rows(): return lax.all_gather(rows, 'heads', axis=0, tiled=True)  176 us
    all_to_all x2, starting transfers between devices, on_device(): lax.all_to_all(sent.reshape((readers, capacity) + sent.shape[1:]), 'pages...  14.2 us
    all_to_all x1, starting transfers between devices, on_device(): lax.all_to_all(asked.reshape(readers, capacity), 'pages', split_axis=0, c...  13.5 us
  transfers between devices with their start and end apart: 7, of which 5 were waited for; matrix products, arithmetic and copies ran while one was open for 3% of the time, Pallas kernels for 0%

commit v1 on v0

--- a/solution.py
+++ b/solution.py
@@ -15,7 +15,14 @@
 
 
 def gather_rows(rows):
-    return lax.all_gather(rows, "heads", axis=0, tiled=True)
+
+    def produce_group(inp, ax_name, row_dim):
+        return jnp.concatenate(
+            lax.all_to_all(jnp.stack([inp for _ in range(lax.axis_size(ax_name))]), ax_name, 0, 0),
+            row_dim,
+        )
+
+    return produce_group(rows, "heads", 0)
 
 
 def scatter_sum(terms):

time: 486 us -> 447 us (0.920)
  waiting for transfers between devices: 402 us -> 293 us
  blocking collectives: 0 us -> 49 us
  starting transfers between devices: 28.1 us -> 48.1 us
  local copies, waits for them, and re-layouts: 13.1 us -> 19.4 us
    all_gather x2 -> x0, waiting for transfers between devices: 176 us -> none  [gather_rows(): return lax.all_gather(rows, 'heads', axis=0, tiled=True)]
    all_to_all x2, waiting for transfers between devices: 0.01 us -> 91.4 us  [on_device(): lax.all_to_all(sent.reshape((readers, capacity) + sent.shape[1:]), 'pages...]
    all_to_all x0 -> x2, blocking collectives: none -> 49 us  [the longest x1 26.8 us: produce_group(): lax.all_to_all(jnp.stack([inp for _ in range(lax.axis_size(ax_name))]), a...]
    reduce_scatter x2, waiting for transfers between devices: 219 us -> 181 us  [scatter_sum(): lax.psum_scatter(terms, 'heads', scatter_dimension=0, tiled=True)]
    all_to_all x2, starting transfers between devices: 14.2 us -> 37.8 us  [on_device(): lax.all_to_all(sent.reshape((readers, capacity) + sent.shape[1:]), 'pages...]
    all_to_all x1, waiting for transfers between devices: 6.83 us -> 20.7 us  [produce_group(): lax.all_to_all(jnp.stack([inp for _ in range(lax.axis_size(ax_name))]), a...]
  transfers between devices with their start and end apart: 7 -> 5, of which waited for: 5 -> 5; matrix products, arithmetic and copies ran while one was open for 3% -> 5% of each run, Pallas kernels for 0% -> 0%
where the time goes in v1:
time: 447 us
  waiting for transfers between devices  293 us (66%)
  blocking collectives  49 us (11%)
  starting transfers between devices  48.1 us (11%)
  local copies, waits for them, and re-layouts  19.4 us (4%)
  between operations  13.8 us (3%)
  other arithmetic  11.8 us (3%)
  matrix products  11.6 us (3%)
    reduce_scatter x2, waiting for transfers between devices, scatter_sum(): lax.psum_scatter(terms, 'heads', scatter_dimension=0, tiled=True)  181 us
    all_to_all x2, waiting for transfers between devices, on_device(): lax.all_to_all(sent.reshape((readers, capacity) + sent.shape[1:]), 'pages...  91.4 us
    all_to_all x2, starting transfers between devices, on_device(): lax.all_to_all(sent.reshape((readers, capacity) + sent.shape[1:]), 'pages...  37.8 us
    all_to_all x1, blocking collectives, produce_group(): lax.all_to_all(jnp.stack([inp for _ in range(lax.axis_size(ax_name))]), a...  26.8 us
    all_to_all x1, blocking collectives, on_device(): lax.all_to_all(asked.reshape(readers, capacity), 'pages', split_axis=0, c...  22.2 us
    all_to_all x1, waiting for transfers between devices, produce_group(): lax.all_to_all(jnp.stack([inp for _ in range(lax.axis_size(ax_name))]), a...  20.7 us
    all_to_all x1, starting transfers between devices, produce_group(): lax.all_to_all(jnp.stack([inp for _ in range(lax.axis_size(ax_name))]), a...  10 us
  transfers between devices with their start and end apart: 5, of which 5 were waited for; matrix products, arithmetic and copies ran while one was open for 5% of the time, Pallas kernels for 0%

profile of v1, /device:TPU:8, one launch (start us, length us, event | category | flops | bytes accessed | tf_op | source)
XLA Modules:
  0.0 446.6 jit_solution(7720646325788906802)
XLA Ops:
  6.5 0.8 copy.31
  7.8 22.2 %all_to_all.29 = s32[64,1,2]{2,1,0:T(1,128)S(1)} all-to-all(s32[64,1,2]{2,1,0:T(1,128)S(1)} %bitcast.71), channel_id=1, replica_groups=mesh['pages'=64,'heads'=8] {'pages'}, dimensions={0} | all-to-all | bytes 1024 | tf_op jit(solution)/shard_map/all_to_all | solution.py:58
  30.1 2.3 stack.4
  32.3 10.0 %all-to-all-start.2 = ((bf16[8,96,1024]{2,1,0:T(8,128)(2,1)}), bf16[8,96,1024]{2,1,0:T(8,128)(2,1)S(1)}, u32[]{:S(2)}, u32[]{:S(2)}) async-start(bf16[8,96,1024]{2,1,0:T(8,128)(2,1)} %stack.4), calls=%async_computation.2 | async-start | bytes 3145728 | tf_op jit(solution)/shard_map/all_to_all | solution.py:21
  42.4 2.9 slice_bitcast_fusion
  46.7 3.4 gather_fusion
  50.1 2.1 gather_fusion.1
  52.2 4.6 %broadcast_select_fusion = (bf16[128,2,32,128]{3,2,1,0:T(8,128)(2,1)}, bf16[128,2,32,128]{3,2,1,0:T(8,128)(2,1)}) fusion(bf16[128,2,32,128]{3,2,1,0:T(8,128)(2,1)} %gather_fusion.1, pred[128]{0:T(512)(128)(4,1)S(1)} %compare_and_fusion.1, bf16[128,2,32,128]{3,2,1,0:T(8,128)(2,1)} %gather_fusion), kind=kLoop, calls=%fused_computation.16 | loop fusion | flops 2097152 | bytes 8388736 | tf_op jit(solution)/shard_map/jit(_take)/select_n | solution.py:63
  56.9 20.7 %all-to-all-done.2 = bf16[8,96,1024]{2,1,0:T(8,128)(2,1)S(1)} async-done(((bf16[8,96,1024]{2,1,0:T(8,128)(2,1)}), bf16[8,96,1024]{2,1,0:T(8,128)(2,1)S(1)}, u32[]{:S(2)}, u32[]{:S(2)}) %all-to-all-start.2) | async-done | bytes 1572896 | tf_op jit(solution)/shard_map/all_to_all | solution.py:21
  77.6 11.3 %all-to-all-start.1 = ((bf16[64,2,2,32,128]{4,3,2,1,0:T(8,128)(2,1)}), bf16[64,2,2,32,128]{4,3,2,1,0:T(8,128)(2,1)}, u32[]{:S(2)}, u32[]{:S(2)}) async-start(bf16[64,2,2,32,128]{4,3,2,1,0:T(8,128)(2,1)} %bitcast.58), calls=%async_computation.1 | async-start | bytes 4194304 | tf_op jit(solution)/shard_map/all_to_all | solution.py:67
  91.1 2.4 fusion.55
  93.5 45.7 %all-to-all-done.1 = bf16[64,2,2,32,128]{4,3,2,1,0:T(8,128)(2,1)} async-done(((bf16[64,2,2,32,128]{4,3,2,1,0:T(8,128)(2,1)}), bf16[64,2,2,32,128]{4,3,2,1,0:T(8,128)(2,1)}, u32[]{:S(2)}, u32[]{:S(2)}) %all-to-all-start.1) | async-done | bytes 2097184 | tf_op jit(solution)/shard_map/all_to_all | solution.py:67
  139.5 2.3 gather_fusion.2
  143.1 2.8 convolution_convert_fusion.1
  146.0 90.2 %reduce-scatter.3.cloned.1.call-done = bf16[96,1024]{1,0:T(8,128)(2,1)} async-done(((bf16[768,1024]{1,0:T(8,128)(2,1)}), bf16[96,1024]{1,0:T(8,128)(2,1)}) %reduce-scatter.3.cloned.1.call-update) | async-done | bytes 196624 | tf_op jit(solution)/shard_map/reduce_scatter | solution.py:29
  236.2 1.0 add_convert_fusion.1
  237.4 26.8 %all_to_all.30 = bf16[8,96,1024]{2,1,0:T(8,128)(2,1)S(1)} all-to-all(bf16[8,96,1024]{2,1,0:T(8,128)(2,1)S(1)} %stack.5), channel_id=1, replica_groups=mesh['pages'=64,'heads'=8] {'heads'}, dimensions={0} | all-to-all | bytes 3145728 | tf_op jit(solution)/shard_map/all_to_all | solution.py:21
  264.2 26.5 %all-to-all-start.3 = ((bf16[64,2,2,32,128]{4,3,2,1,0:T(8,128)(2,1)}), bf16[64,2,2,32,128]{4,3,2,1,0:T(8,128)(2,1)}, u32[]{:S(2)}, u32[]{:S(2)}) async-start(bf16[64,2,2,32,128]{4,3,2,1,0:T(8,128)(2,1)} %bitcast.57), calls=%async_computation.4 | async-start | bytes 4194304 | tf_op jit(solution)/shard_map/all_to_all | solution.py:67
  292.8 2.4 fusion.56
  295.2 45.7 %all-to-all-done.3 = bf16[64,2,2,32,128]{4,3,2,1,0:T(8,128)(2,1)} async-done(((bf16[64,2,2,32,128]{4,3,2,1,0:T(8,128)(2,1)}), bf16[64,2,2,32,128]{4,3,2,1,0:T(8,128)(2,1)}, u32[]{:S(2)}, u32[]{:S(2)}) %all-to-all-start.3) | async-done | bytes 2097184 | tf_op jit(solution)/shard_map/all_to_all | solution.py:67
  341.2 2.3 gather_fusion.3
  344.9 2.8 convolution_convert_fusion
  347.6 90.4 %reduce-scatter.5.cloned.1.call-done = bf16[96,1024]{1,0:T(8,128)(2,1)} async-done(((bf16[768,1024]{1,0:T(8,128)(2,1)}), bf16[96,1024]{1,0:T(8,128)(2,1)}) %reduce-scatter.5.cloned.1.call-update) | async-done | bytes 196624 | tf_op jit(solution)/shard_map/reduce_scatter | solution.py:29
  438.1 1.7 add_convert_fusion
  (67 shorter events, 9.4 us)
Async XLA Ops:
  32.3 45.3 %all-to-all-start.2 = ((bf16[8,96,1024]{2,1,0:T(8,128)(2,1)}), bf16[8,96,1024]{2,1,0:T(8,128)(2,1)S(1)}, u32[]{:S(2)}, u32[]{:S(2)}) async-start(bf16[8,96,1024]{2,1,0:T(8,128)(2,1)} %stack.4), calls=%async_computation.2 | async-start | bytes 3145728 | tf_op jit(solution)/shard_map/all_to_all | solution.py:21
  77.6 11.4 %copy-start.2 = (s32[16]{0:T(128)S(1)}, s32[16]{0:T(128)}, u32[]{:S(2)}) copy-start(s32[16]{0:T(128)} %param.15) | copy-start | bytes 196
  77.6 61.6 %all-to-all-start.1 = ((bf16[64,2,2,32,128]{4,3,2,1,0:T(8,128)(2,1)}), bf16[64,2,2,32,128]{4,3,2,1,0:T(8,128)(2,1)}, u32[]{:S(2)}, u32[]{:S(2)}) async-start(bf16[64,2,2,32,128]{4,3,2,1,0:T(8,128)(2,1)} %bitcast.58), calls=%async_computation.1 | async-start | bytes 4194304 | tf_op jit(solution)/shard_map/all_to_all | solution.py:67
  88.9 147.3 %reduce-scatter.3.cloned.1.call-start = ((), (), s32[]{:S(2)}) async-start(), calls=%async_computation.7 | async-start | bytes 1769472 | tf_op jit(solution)/shard_map/reduce_scatter | solution.py:29
  89.5 1.6 copy-start.3
  142.1 1.0 copy-start.1
  143.1 93.1 %copy-start = (bf16[96,1024]{1,0:T(8,128)(2,1)S(1)}, bf16[96,1024]{1,0:T(8,128)(2,1)}, u32[]{:S(2)}) copy-start(bf16[96,1024]{1,0:T(8,128)(2,1)} %param.10) | copy-start | bytes 589828
  264.2 76.8 %all-to-all-start.3 = ((bf16[64,2,2,32,128]{4,3,2,1,0:T(8,128)(2,1)}), bf16[64,2,2,32,128]{4,3,2,1,0:T(8,128)(2,1)}, u32[]{:S(2)}, u32[]{:S(2)}) async-start(bf16[64,2,2,32,128]{4,3,2,1,0:T(8,128)(2,1)} %bitcast.57), calls=%async_computation.4 | async-start | bytes 4194304 | tf_op jit(solution)/shard_map/all_to_all | solution.py:67
  290.7 147.4 %reduce-scatter.5.cloned.1.call-start = ((), (), s32[]{:S(2)}) async-start(), calls=%async_computation.8 | async-start | bytes 1769472 | tf_op jit(solution)/shard_map/reduce_scatter | solution.py:29
  291.2 1.6 copy-start.4
Sparse Core Ops, SparseCore 0:
  146.1 90.0 reduce-scatter.2
  347.8 90.2 reduce-scatter.4
